TPU v7x, 32 devices: a whole 2x2x4 slice. The times are simulated.
32 devices in a mesh: pb: 8 (over z, y), ka: 4 (over x, core).
Axes of the slice: x: 2, y: 2, z: 4, core: 2. Of those that a mesh axis runs over, the one named last changes fastest.
Arguments:
- query_rows: bfloat16 [4096, 512], P(('pb', 'ka')), may hold values from -8 to 8
- key_rows: bfloat16 [4096, 128], P(('pb', 'ka')), may hold values from -3 to 3
- value_rows: bfloat16 [4096, 128], P(('pb', 'ka')), may hold values from -6 to 6
- outputs: bfloat16 [4096, 512], P(('pb', 'ka')), may hold values from -3 to 3
- out_grads: bfloat16 [4096, 512], P(('pb', 'ka')), may hold values from -6 to 6
- log_totals: float32 [4, 4096], P(None, ('pb', 'ka'))
- selected: int32 [32, 2], P(('pb', 'ka')), may hold values from 0 to 31, as said below
- counts: int32 [32], P(('pb', 'ka')), may hold values from 1 to 2, as said below
Outputs:
- query_grad: float32 [4096, 512], P(('pb', 'ka'))
- key_grad: float32 [4096, 128], P(('pb', 'ka'))
- value_grad: float32 [4096, 128], P(('pb', 'ka'))
Inputs may be any that keep to these rules, and one draw needn't show every extreme that they name: `selected`: slot 0 of row q is q itself; the first counts[q] entries of row q are distinct blocks no later than q; entries from slot counts[q] on are padding and are ignored. counts[q] is at most q + 1; the last query block's count is 2.
All inputs are finite; a program needn't handle non-finite values.
Results may differ from a plain program's by a relative error of at most 0.0029.
Values may be sent and summed in bfloat16 or wider, within the bound.
A program may use at most 64 MiB of HBM per device.

v0:
```python
import jax
import jax.numpy as jnp
from jax import lax
from jax.sharding import PartitionSpec as P

VERY_LOW = -1e30


def passed_along(value, axis, steps):
    count = lax.axis_size(axis)
    pairs = [(source, (source + steps) % count) for source in range(count)]
    return lax.ppermute(value, axis, pairs)


def head_sums(grad_rows, out_rows, head_width):
    row_total = grad_rows.shape[0]
    part_heads = grad_rows.shape[1] // head_width
    product = grad_rows.astype(jnp.float32) * out_rows.astype(jnp.float32)
    return jnp.sum(product.reshape(row_total, part_heads, head_width), axis=2).T


def shards(query_rows, key_rows, value_rows, outputs, out_grads, log_totals, selected, counts):
    ka_count = lax.axis_size("ka")
    ka_index = lax.axis_index("ka")
    pb_index = lax.axis_index("pb")
    block_count = selected.shape[0]
    slot_count = selected.shape[1]
    head_width = key_rows.shape[1]
    block_rows = query_rows.shape[0] // block_count
    score_scale = head_width ** (-0.5)
    key_pairs = jnp.concatenate([key_rows, value_rows], 1)
    column_keys = lax.all_gather(key_pairs, "pb", axis=0, tiled=True)
    peer_slots, peer_counts = (
        lax.all_gather(selected, "ka", axis=0, tiled=True),
        lax.all_gather(counts, "ka", axis=0, tiled=True),
    )
    key_grads = jnp.zeros((column_keys.shape[0], 2 * head_width), jnp.float32)
    row_offsets = jnp.arange(block_rows, dtype=jnp.int32)
    flat_owner = jnp.repeat(jnp.arange(block_count, dtype=jnp.int32), slot_count)
    flat_slot = jnp.tile(jnp.arange(slot_count, dtype=jnp.int32), block_count)
    flat_places = jnp.arange(block_count * slot_count, dtype=jnp.int32)

    def visit_block(row_stack, query_grad, stat_stack, anchor, key_grads):
        held_query = row_stack[0]
        held_grad = row_stack[1]
        total_rows = stat_stack[0]
        delta_rows = head_sums(row_stack[1], row_stack[2], head_width)
        part_heads = total_rows.shape[0]
        held_slots = lax.dynamic_slice_in_dim(
            peer_slots, anchor * block_count, block_count, 0
        ).reshape(-1)
        held_counts = jnp.repeat(
            lax.dynamic_slice_in_dim(peer_counts, anchor * block_count, block_count, 0), slot_count
        )
        first_block = (pb_index * ka_count + anchor) * block_count
        wanted = (flat_slot < held_counts) & (held_slots // block_count % ka_count == ka_index)
        position = jnp.cumsum(wanted.astype(jnp.int32)) - 1
        placed = wanted[:, None] & (position[:, None] == flat_places[None, :])
        packed_ids = jnp.sum(jnp.where(placed, held_slots[:, None], 0), axis=0)
        packed_owner = jnp.sum(jnp.where(placed, flat_owner[:, None], 0), axis=0)
        live_tiles = jnp.sum(wanted.astype(jnp.int32))

        def one_tile(tile_index, loop_state):
            query_grad, key_grads = loop_state
            key_block = packed_ids[tile_index]
            owner_block = packed_owner[tile_index]
            key_start = (
                key_block // (block_count * ka_count) * block_count + key_block % block_count
            ) * block_rows
            pair_tile = lax.dynamic_slice_in_dim(column_keys, key_start, block_rows, 0)
            key_tile = pair_tile[:, :head_width]
            value_tile = pair_tile[:, head_width:]
            query_tile = held_query.reshape(block_rows, part_heads, head_width)
            grad_tile = held_grad.reshape(block_rows, part_heads, head_width)
            scores = (
                jnp.einsum("rhd,cd->hrc", query_tile, key_tile, preferred_element_type=jnp.float32)
                * score_scale
            )
            query_pos = (first_block + owner_block) * block_rows + row_offsets
            key_pos = key_block * block_rows + row_offsets
            allowed = key_pos[None, :] <= query_pos[:, None]
            probs_full = jnp.exp(
                jnp.where(allowed[None], scores - total_rows[:, :, None], VERY_LOW)
            )
            prob_grads = jnp.einsum(
                "rhd,cd->hrc", grad_tile, value_tile, preferred_element_type=jnp.float32
            )
            score_grads = probs_full * (prob_grads - delta_rows[:, :, None])
            rounded_probs = probs_full.astype(jnp.bfloat16)
            rounded_grads = score_grads.astype(jnp.bfloat16)
            value_part = jnp.einsum(
                "hrc,rhd->cd", rounded_probs, grad_tile, preferred_element_type=jnp.float32
            )
            key_part = (
                jnp.einsum(
                    "hrc,rhd->cd", rounded_grads, query_tile, preferred_element_type=jnp.float32
                )
                * score_scale
            )
            query_part = (
                jnp.einsum(
                    "hrc,cd->rhd", rounded_grads, key_tile, preferred_element_type=jnp.float32
                )
                * score_scale
            )
            old_query = query_grad
            query_grad = old_query + query_part.reshape(block_rows, -1)
            old_keys = lax.dynamic_slice_in_dim(key_grads, key_start, block_rows, 0)
            key_grads = lax.dynamic_update_slice_in_dim(
                key_grads, old_keys + jnp.concatenate([key_part, value_part], 1), key_start, 0
            )
            return (query_grad, key_grads)

        return lax.fori_loop(0, live_tiles, one_tile, (query_grad, key_grads))

    query_part = query_rows
    grad_zero = jnp.zeros(query_part.shape, jnp.float32)
    row_stack = jnp.stack([query_part, out_grads, outputs])
    query_grad = grad_zero
    stat_stack = log_totals[None]

    def forward_hop(hop_index, loop_state):
        row_stack, query_grad, stat_stack, key_grads = loop_state
        anchor = (ka_index - hop_index) % ka_count
        query_grad, key_grads = visit_block(row_stack, query_grad, stat_stack, anchor, key_grads)
        row_stack = passed_along(row_stack, "ka", 1)
        query_grad, stat_stack = passed_along((query_grad, stat_stack), "ka", 1)
        return (row_stack, query_grad, stat_stack, key_grads)

    row_stack, query_grad, stat_stack, key_grads = lax.fori_loop(
        0, ka_count - 1, forward_hop, (row_stack, query_grad, stat_stack, key_grads)
    )
    query_grad, key_grads = visit_block(
        row_stack, query_grad, stat_stack, (ka_index + 1) % ka_count, key_grads
    )
    query_grad = passed_along(query_grad, "ka", 1)
    owned_grads = lax.psum_scatter(key_grads, "pb", scatter_dimension=0, tiled=True)
    return (query_grad, owned_grads[:, :head_width], owned_grads[:, head_width:])


def solution(mesh):
    return jax.shard_map(
        shards,
        mesh=mesh,
        in_specs=(
            P(("pb", "ka"), None),
            P(("pb", "ka"), None),
            P(("pb", "ka"), None),
            P(("pb", "ka"), None),
            P(("pb", "ka"), None),
            P(None, ("pb", "ka")),
            P(("pb", "ka"), None),
            P(("pb", "ka")),
        ),
        out_specs=(P(("pb", "ka"), None), P(("pb", "ka"), None), P(("pb", "ka"), None)),
        check_vma=False,
    )
```

profile of v0, /device:TPU:0, one launch (start us, length us, event | category | flops | bytes accessed | tf_op | source)
XLA Modules:
  0.0 184.5 jit_solution(7212830723820672716)
XLA Ops:
  7.9 0.6 copy-done.6
  8.5 0.7 dynamic-slice
  9.2 0.8 dynamic-update-slice
  10.0 6.4 %all-reduce = s32[4]{0:T(128)S(1)} all-reduce(s32[4]{0:T(128)S(1)} %dynamic-update-slice), channel_id=1, replica_groups=mesh['pb'=8,'ka'=4] {'ka'}, use_global_device_ids=true, to_apply=%add | all-reduce | flops 4 | bytes 32
  16.4 0.7 copy-done.5
  17.0 5.0 %all-gather = s32[4,1,2]{2,1,0:T(1,128)S(1)} all-gather(s32[1,1,2]{2,1,0:T(1,128)S(1)} %bitcast.222), channel_id=1, replica_groups=mesh['pb'=8,'ka'=4] {'ka'}, dimensions={0}, use_global_device_ids=true | all-gather | bytes 40 | tf_op jit(solution)/shard_map/all_gather | solution.py:34
  22.1 0.6 dynamic_slice.84
  22.7 1.3 convert_reduce_fusion.1
  23.9 0.6 and_convert_fusion
  24.5 1.1 copy.63
  25.7 0.8 copy-done.2
  26.6 0.6 copy-done.3
  27.3 31.9 %all_gather.11 = bf16[1024,256]{1,0:T(8,128)(2,1)S(1)} all-gather(bf16[128,256]{1,0:T(8,128)(2,1)S(1)} %pad_maximum_fusion.1), channel_id=1, replica_groups=mesh['pb'=8,'ka'=4] {'pb'}, dimensions={0}, use_global_device_ids=true | all-gather | bytes 589824 | tf_op jit(solution)/shard_map/all_gather | solution.py:32
  59.4 0.6 copy-done
  60.0 40.6 %while.86 = (s32[]{:T(128)}, bf16[3,128,512]{1,2,0:T(8,128)(2,1)S(1)}, f32[128,512]{0,1:T(8,128)S(1)}, f32[1,4,128]{2,1,0:T(4,128)S(1)}, f32[1024,256]{0,1:T(8,1...) while((s32[]{:T(128)}, ...), condition=%wide.region_7.8_spmd.clone.clone, body=%wide.region_0.7_spmd.clone.clone.sunk | while | flops 84836216 | bytes 8673559 | solution.py:130
  60.1 0.7 dynamic_slice.117
  60.7 1.3 convert_reduce_fusion.3
  62.0 0.6 fusion.81
  63.1 6.2 %while.88 = (s32[]{:T(128)}, f32[128,512]{0,1:T(8,128)S(1)}, f32[1024,256]{0,1:T(8,128)S(1)}, s32[]{:T(128)}, s32[2]{0:T(128)S(1)}, /*index=5*/bf16[1024,256]{1,...) while((s32[]{:T(128)}, f32[128,512]{0,1:T(8,128)S(1)}, ...), condition=%wide.region_6.6_spmd.clone, body=%wide.region_5.5_spmd.clone.sunk | while | flops 84574488 | bytes 3415011 | solution.py:114
  63.7 0.6 dynamic_slice.121
  67.5 0.2 fusion.102
  67.9 0.2 convolution_multiply_fusion.7
  68.2 0.2 convolution_bitcast_fusion.9
  68.4 0.2 fusion.104
  69.3 1.0 collective-permute-start.1
  70.3 4.8 %collective-permute-done.1 = f32[128,512]{0,1:T(8,128)S(1)} collective-permute-done((f32[128,512]{0,1:T(8,128)S(1)}, f32[128,512]{0,1:T(8,128)S(1)}, u32[]{:S(2)}, u32[]{:S(2)}) %collective-permute-start.1) | collective-permute-done | bytes 262176 | tf_op jit(solution)/shard_map/while/body/eval_jaxpr/ppermute | solution.py:12
  75.3 0.7 dynamic_slice.117
  76.0 1.3 convert_reduce_fusion.3
  77.3 0.6 fusion.81
  78.3 6.2 %while.88 = (s32[]{:T(128)}, f32[128,512]{0,1:T(8,128)S(1)}, f32[1024,256]{0,1:T(8,128)S(1)}, s32[]{:T(128)}, s32[2]{0:T(128)S(1)}, /*index=5*/bf16[1024,256]{1,...) while((s32[]{:T(128)}, f32[128,512]{0,1:T(8,128)S(1)}, ...), condition=%wide.region_6.6_spmd.clone, body=%wide.region_5.5_spmd.clone.sunk | while | flops 84574488 | bytes 3415011 | solution.py:114
  78.9 0.6 dynamic_slice.121
  82.8 0.2 fusion.102
  83.1 0.2 convolution_multiply_fusion.7
  83.4 0.2 convolution_bitcast_fusion.9
  83.6 0.2 fusion.104
  84.6 5.7 %collective-permute-done.1 = f32[128,512]{0,1:T(8,128)S(1)} collective-permute-done((f32[128,512]{0,1:T(8,128)S(1)}, f32[128,512]{0,1:T(8,128)S(1)}, u32[]{:S(2)}, u32[]{:S(2)}) %collective-permute-start.1) | collective-permute-done | bytes 262176 | tf_op jit(solution)/shard_map/while/body/eval_jaxpr/ppermute | solution.py:12
  90.5 0.7 dynamic_slice.117
  91.2 1.3 convert_reduce_fusion.3
  92.5 0.6 fusion.81
  93.5 0.6 while.88
  94.3 6.2 %collective-permute-done.1 = f32[128,512]{0,1:T(8,128)S(1)} collective-permute-done((f32[128,512]{0,1:T(8,128)S(1)}, f32[128,512]{0,1:T(8,128)S(1)}, u32[]{:S(2)}, u32[]{:S(2)}) %collective-permute-start.1) | collective-permute-done | bytes 262176 | tf_op jit(solution)/shard_map/while/body/eval_jaxpr/ppermute | solution.py:12
  100.9 0.7 while.87
  101.6 1.3 copy.67
  103.1 2.6 %collective-permute-start.3 = (f32[128,512]{1,0:T(8,128)S(1)}, f32[128,512]{1,0:T(8,128)S(1)}, u32[]{:S(2)}, u32[]{:S(2)}) collective-permute-start(f32[128,512]{1,0:T(8,128)S(1)} %copy.66), channel_id=1, source_target_pairs={{0,1},{1,2},{2,3},{3,0},{4,5},{5,6},{6,7},{7,4},{8,9},{9,10},{10,1... | collective-permute-start | bytes 786440 | tf_op jit(solution)/shard_map/ppermute | solution.py:12
  105.7 3.3 %collective-permute-done.3 = f32[128,512]{1,0:T(8,128)S(1)} collective-permute-done((f32[128,512]{1,0:T(8,128)S(1)}, f32[128,512]{1,0:T(8,128)S(1)}, u32[]{:S(2)}, u32[]{:S(2)}) %collective-permute-start.3) | collective-permute-done | bytes 262176 | tf_op jit(solution)/shard_map/ppermute | solution.py:12
  109.0 66.4 %reduce-scatter.2.cloned.1.call-done = f32[128,256]{1,0:T(8,128)} async-done(((f32[1024,256]{1,0:T(8,128)}), f32[128,256]{1,0:T(8,128)}) %reduce-scatter.2.cloned.1.call-update) | async-done | bytes 131088 | tf_op jit(solution)/shard_map/reduce_scatter | solution.py:137
  175.4 1.5 fusion.43
  176.9 0.7 copy.125
  (79 shorter events, 3.4 us)
Async XLA Ops:
  7.2 168.3 %reduce-scatter.2.cloned.1.call-start = ((), (), s32[]{:S(2)}) async-start(), calls=%async_computation.1 | async-start | bytes 1179648 | tf_op jit(solution)/shard_map/reduce_scatter | solution.py:137
  7.9 0.7 copy-start.6
  16.4 0.7 copy-start.5
  24.5 1.1 copy-start.1
  25.6 0.9 copy-start.2
  26.5 0.8 copy-start.3
  26.5 0.8 copy-start.4
  59.3 0.7 copy-start
  60.0 15.2 %collective-permute-start = (bf16[3,128,512]{1,2,0:T(8,128)(2,1)S(1)}, bf16[3,128,512]{1,2,0:T(8,128)(2,1)S(1)}, u32[]{:S(2)}, u32[]{:S(2)}) collective-permute-start(bf16[3,128,512]{1,2,0:T(8,128)(2,1)S(1)} %copy.101), channel_id=1, source_target_pairs={{0,1},{1,2},{2,3},{3,0},{4,5},{5,6},{6,7},{7,4},{8,9},{9,10},{10,1... | collective-permute-start | bytes 1179656 | tf_op jit(solution)/shard_map/while/body/eval_jaxpr/ppermute | solution.py:12
  69.3 5.8 %collective-permute-start.1 = (f32[128,512]{0,1:T(8,128)S(1)}, f32[128,512]{0,1:T(8,128)S(1)}, u32[]{:S(2)}, u32[]{:S(2)}) collective-permute-start(f32[128,512]{0,1:T(8,128)S(1)} %get-tuple-element.1444), channel_id=1, source_target_pairs={{0,1},{1,2},{2,3},{3,0},{4,5},{5,6},{6,7},{7,4},{8,9},{9,10},{10,1... | collective-permute-start | bytes 786440 | tf_op jit(solution)/shard_map/while/body/eval_jaxpr/ppermute | solution.py:12
  70.3 4.9 %collective-permute-start.2 = (f32[1,4,128]{2,1,0:T(4,128)S(1)}, f32[1,4,128]{2,1,0:T(4,128)S(1)}, u32[]{:S(2)}, u32[]{:S(2)}) collective-permute-start(f32[1,4,128]{2,1,0:T(4,128)S(1)} %get-tuple-element.1678), channel_id=1, source_target_pairs={{0,1},{1,2},{2,3},{3,0},{4,5},{5,6},{6,7},{7,4},{8,9},{9,10},{10,1... | collective-permute-start | bytes 6152 | tf_op jit(solution)/shard_map/while/body/eval_jaxpr/ppermute | solution.py:12
  75.2 15.2 %collective-permute-start = (bf16[3,128,512]{1,2,0:T(8,128)(2,1)S(1)}, bf16[3,128,512]{1,2,0:T(8,128)(2,1)S(1)}, u32[]{:S(2)}, u32[]{:S(2)}) collective-permute-start(bf16[3,128,512]{1,2,0:T(8,128)(2,1)S(1)} %copy.101), channel_id=1, source_target_pairs={{0,1},{1,2},{2,3},{3,0},{4,5},{5,6},{6,7},{7,4},{8,9},{9,10},{10,1... | collective-permute-start | bytes 1179656 | tf_op jit(solution)/shard_map/while/body/eval_jaxpr/ppermute | solution.py:12
  84.5 5.8 %collective-permute-start.1 = (f32[128,512]{0,1:T(8,128)S(1)}, f32[128,512]{0,1:T(8,128)S(1)}, u32[]{:S(2)}, u32[]{:S(2)}) collective-permute-start(f32[128,512]{0,1:T(8,128)S(1)} %get-tuple-element.1444), channel_id=1, source_target_pairs={{0,1},{1,2},{2,3},{3,0},{4,5},{5,6},{6,7},{7,4},{8,9},{9,10},{10,1... | collective-permute-start | bytes 786440 | tf_op jit(solution)/shard_map/while/body/eval_jaxpr/ppermute | solution.py:12
  84.6 5.8 %collective-permute-start.2 = (f32[1,4,128]{2,1,0:T(4,128)S(1)}, f32[1,4,128]{2,1,0:T(4,128)S(1)}, u32[]{:S(2)}, u32[]{:S(2)}) collective-permute-start(f32[1,4,128]{2,1,0:T(4,128)S(1)} %get-tuple-element.1678), channel_id=1, source_target_pairs={{0,1},{1,2},{2,3},{3,0},{4,5},{5,6},{6,7},{7,4},{8,9},{9,10},{10,1... | collective-permute-start | bytes 6152 | tf_op jit(solution)/shard_map/while/body/eval_jaxpr/ppermute | solution.py:12
  90.4 10.1 %collective-permute-start = (bf16[3,128,512]{1,2,0:T(8,128)(2,1)S(1)}, bf16[3,128,512]{1,2,0:T(8,128)(2,1)S(1)}, u32[]{:S(2)}, u32[]{:S(2)}) collective-permute-start(bf16[3,128,512]{1,2,0:T(8,128)(2,1)S(1)} %copy.101), channel_id=1, source_target_pairs={{0,1},{1,2},{2,3},{3,0},{4,5},{5,6},{6,7},{7,4},{8,9},{9,10},{10,1... | collective-permute-start | bytes 1179656 | tf_op jit(solution)/shard_map/while/body/eval_jaxpr/ppermute | solution.py:12
  94.2 6.3 %collective-permute-start.1 = (f32[128,512]{0,1:T(8,128)S(1)}, f32[128,512]{0,1:T(8,128)S(1)}, u32[]{:S(2)}, u32[]{:S(2)}) collective-permute-start(f32[128,512]{0,1:T(8,128)S(1)} %get-tuple-element.1444), channel_id=1, source_target_pairs={{0,1},{1,2},{2,3},{3,0},{4,5},{5,6},{6,7},{7,4},{8,9},{9,10},{10,1... | collective-permute-start | bytes 786440 | tf_op jit(solution)/shard_map/while/body/eval_jaxpr/ppermute | solution.py:12
  94.2 6.3 %collective-permute-start.2 = (f32[1,4,128]{2,1,0:T(4,128)S(1)}, f32[1,4,128]{2,1,0:T(4,128)S(1)}, u32[]{:S(2)}, u32[]{:S(2)}) collective-permute-start(f32[1,4,128]{2,1,0:T(4,128)S(1)} %get-tuple-element.1678), channel_id=1, source_target_pairs={{0,1},{1,2},{2,3},{3,0},{4,5},{5,6},{6,7},{7,4},{8,9},{9,10},{10,1... | collective-permute-start | bytes 6152 | tf_op jit(solution)/shard_map/while/body/eval_jaxpr/ppermute | solution.py:12
  103.1 5.8 %collective-permute-start.3 = (f32[128,512]{1,0:T(8,128)S(1)}, f32[128,512]{1,0:T(8,128)S(1)}, u32[]{:S(2)}, u32[]{:S(2)}) collective-permute-start(f32[128,512]{1,0:T(8,128)S(1)} %copy.66), channel_id=1, source_target_pairs={{0,1},{1,2},{2,3},{3,0},{4,5},{5,6},{6,7},{7,4},{8,9},{9,10},{10,1... | collective-permute-start | bytes 786440 | tf_op jit(solution)/shard_map/ppermute | solution.py:12
Sparse Core Ops, SparseCore 0:
  103.1 72.2 reduce-scatter.1
where the time goes:
time: 184 us
  waiting for transfers between devices  86.5 us (47%)
  blocking collectives  43.3 us (24%)
  between operations  14.8 us (8%)
  local copies, waits for them, and re-layouts  13.8 us (8%)
  loops' own time  10.6 us (6%)
  other arithmetic  9.41 us (5%)
  starting transfers between devices  4.04 us (2%)
  matrix products  1.93 us (1%)
    reduce_scatter x1, waiting for transfers between devices, shards(): lax.psum_scatter(key_grads, 'pb', scatter_dimension=0, tiled=True)  66.4 us
    all_gather x1, blocking collectives, shards(): column_keys = lax.all_gather(key_pairs, 'pb', axis=0, tiled=True)  31.9 us
    ppermute x10, waiting for transfers between devices, passed_along(): return lax.ppermute(value, axis, pairs)  20 us
    another operation x4, loops' own time, visit_block(): return lax.fori_loop(0, live_tiles, one_tile, (query_grad, key_grads))  10.3 us
    unnamed x21, local copies, waits for them, and re-layouts  6.74 us
    unnamed x1, blocking collectives  6.38 us
    reduce_sum x4, other arithmetic, visit_block(): live_tiles = jnp.sum(wanted.astype(jnp.int32))  5.18 us
    all_gather x1, blocking collectives, shards(): lax.all_gather(selected, 'ka', axis=0, tiled=True)  5.05 us
  transfers between devices with their start and end apart: 11, of which 5 were waited for; matrix products, arithmetic and copies ran while one was open for 7% of the time, Pallas kernels for 0%

commit v1 on v0

--- a/solution.py
+++ b/solution.py
@@ -1,6 +1,10 @@
+import functools
+
 import jax
 import jax.numpy as jnp
 from jax import lax
+from jax.experimental import pallas as pl
+from jax.experimental.pallas import tpu as pltpu
 from jax.sharding import PartitionSpec as P
 
 VERY_LOW = -1e30
@@ -138,9 +142,255 @@
     return (query_grad, owned_grads[:, :head_width], owned_grads[:, head_width:])
 
 
+MESH = pl.DeviceIdType.MESH
+VMEM_BUDGET = 40 << 20
+
+
+def tile_grads(key_tile, value_tile, query_stack, grad_stack, total_row, delta_row, allowed, scale):
+    nt = (((1,), (1,)), ((), ()))
+    scores = lax.dot_general(key_tile, query_stack, nt, preferred_element_type=jnp.float32) * scale
+    probs = jnp.exp(jnp.where(allowed, scores - total_row, VERY_LOW))
+    prob_grads = lax.dot_general(value_tile, grad_stack, nt, preferred_element_type=jnp.float32)
+    score_grads = (probs * (prob_grads - delta_row)).astype(jnp.bfloat16)
+    value_part = jnp.dot(probs.astype(jnp.bfloat16), grad_stack, preferred_element_type=jnp.float32)
+    key_part = jnp.dot(score_grads, query_stack, preferred_element_type=jnp.float32) * scale
+    query_part = (
+        lax.dot_general(
+            score_grads, key_tile, (((0,), (0,)), ((), ())), preferred_element_type=jnp.float32
+        )
+        * scale
+    )
+    return query_part, key_part, value_part
+
+
+def whole_kernel(
+    ka_count, inner, line_count, extra,
+    query_ref, key_ref, value_ref, out_ref, grad_ref, total_ref, selected_ref, counts_ref,
+    query_grad_ref, key_grad_ref, value_grad_ref,
+    plane_kv, line_kv, line_kv_out, plane_part, line_part, line_part_out,
+    plane_info, line_info, query_stack, grad_stack, query_acc, key_acc, value_acc,
+    info_send_p, info_recv_p, info_send_l, info_recv_l,
+    kv_send_p, kv_recv_p, kv_send_l, kv_recv_l,
+    part_send_p, part_recv_p, part_send_l, part_recv_l, load_sem,
+):
+    plane_count = inner * ka_count
+    pb_index, ka_index = lax.axis_index("pb"), lax.axis_index("ka")
+    line = lax.div(pb_index, inner)
+    row = lax.rem(pb_index, inner)
+    place = row * ka_count + ka_index
+    block_rows, head_width = key_ref.shape
+    heads = total_ref.shape[0]
+    scale = head_width ** (-0.5)
+    block = line * plane_count + place
+
+    loads = [
+        pltpu.make_async_copy(key_ref, plane_kv.at[place, pl.ds(0, block_rows)], load_sem.at[0]),
+        pltpu.make_async_copy(value_ref, plane_kv.at[place, pl.ds(block_rows, block_rows)], load_sem.at[1]),
+    ]
+    for load in loads:
+        load.start()
+
+    def plane_peer(offset):
+        peer = lax.rem(place + offset, plane_count)
+        return peer, (line * inner + lax.div(peer, ka_count), lax.rem(peer, ka_count))
+
+    def line_peer(offset):
+        peer = lax.rem(line + offset, line_count)
+        return peer, (peer * inner + row, ka_index)
+
+    barrier = pltpu.get_barrier_semaphore()
+    for offset in range(1, plane_count):
+        pl.semaphore_signal(barrier, inc=1, device_id=plane_peer(offset)[1], device_id_type=MESH)
+    for offset in range(1, line_count):
+        pl.semaphore_signal(barrier, inc=1, device_id=line_peer(offset)[1], device_id_type=MESH)
+
+    targets = [
+        jnp.where(slot + 1 < counts_ref[0], selected_ref[0, slot + 1], -1) for slot in range(extra)
+    ]
+    for slot in range(extra):
+        lines = jnp.full((8, 128), targets[slot], jnp.int32)
+        plane_info[place, slot] = lines
+        line_info[line, slot] = lines
+    for load in loads:
+        load.wait()
+    pl.semaphore_wait(barrier, plane_count + line_count - 2)
+
+    def exchange(peer_of, count, me, source_of, target, send, recv):
+        copies = []
+        for offset in range(1, count):
+            peer, device = peer_of(offset)
+            copy = pltpu.make_async_remote_copy(
+                src_ref=source_of(peer), dst_ref=target.at[me], send_sem=send.at[offset],
+                recv_sem=recv.at[me], device_id=device, device_id_type=MESH,
+            )
+            copy.start()
+            copies.append(copy)
+        return copies
+
+    def arrive(peer_of, count, target, send, recv):
+        for offset in range(1, count):
+            peer, device = peer_of(offset)
+            pltpu.make_async_remote_copy(
+                src_ref=target.at[peer], dst_ref=target.at[peer], send_sem=send.at[offset],
+                recv_sem=recv.at[peer], device_id=device, device_id_type=MESH,
+            ).wait_recv()
+
+    sent = []
+    sent += exchange(line_peer, line_count, line, lambda p: line_info.at[line], line_info, info_send_l, info_recv_l)
+    sent += exchange(plane_peer, plane_count, place, lambda p: plane_info.at[place], plane_info, info_send_p, info_recv_p)
+    sent += exchange(plane_peer, plane_count, place, lambda p: plane_kv.at[place], plane_kv, kv_send_p, kv_recv_p)
+
+    deltas = []
+    for head in range(heads):
+        columns = pl.ds(head * head_width, head_width)
+        rows = pl.ds(head * block_rows, block_rows)
+        query_stack[rows, :] = query_ref[:, columns]
+        grad_stack[rows, :] = grad_ref[:, columns]
+        product = grad_ref[:, columns].astype(jnp.float32) * out_ref[:, columns].astype(jnp.float32)
+        deltas.append(jnp.sum(product.T, axis=0, keepdims=True))
+    delta_row = jnp.concatenate(deltas, axis=1)
+    total_row = jnp.concatenate([total_ref[head : head + 1, :] for head in range(heads)], axis=1)
+    stack_shape = (block_rows, heads * block_rows)
+    key_offset = lax.broadcasted_iota(jnp.int32, stack_shape, 0)
+    query_offset = lax.rem(lax.broadcasted_iota(jnp.int32, stack_shape, 1), block_rows)
+
+    arrive(line_peer, line_count, line_info, info_send_l, info_recv_l)
+    arrive(plane_peer, plane_count, plane_info, info_send_p, info_recv_p)
+    arrive(plane_peer, plane_count, plane_kv, kv_send_p, kv_recv_p)
+
+    for offset in range(line_count):
+        peer, _ = line_peer(offset)
+        for slot in range(extra):
+            wanted = line_info[peer, slot][0:1, :]
+            picked = jnp.zeros(plane_kv.shape[1:], jnp.float32)
+            for other in range(plane_count):
+                picked = jnp.where(
+                    wanted == line * plane_count + other, plane_kv[other].astype(jnp.float32), picked
+                )
+            if offset == 0:
+                line_kv[line, slot] = picked.astype(jnp.bfloat16)
+            else:
+                line_kv_out[peer, slot] = picked.astype(jnp.bfloat16)
+    sent += exchange(line_peer, line_count, line, lambda p: line_kv_out.at[p], line_kv, kv_send_l, kv_recv_l)
+
+    query_part, key_part, value_part = tile_grads(
+        key_ref[...], value_ref[...], query_stack[...], grad_stack[...], total_row, delta_row,
+        key_offset <= query_offset, scale,
+    )
+    query_acc[...] = query_part
+    key_acc[...] = key_part
+    value_acc[...] = value_part
+
+    arrive(line_peer, line_count, line_kv, kv_send_l, kv_recv_l)
+    for slot in range(extra):
+        source = lax.div(jnp.maximum(targets[slot], 0), plane_count)
+        pair = line_kv[source, slot]
+        allowed = (key_offset + targets[slot] * block_rows <= query_offset + block * block_rows) & (
+            jnp.full(stack_shape, targets[slot], jnp.int32) >= 0
+        )
+        query_part, key_part, value_part = tile_grads(
+            pair[:block_rows], pair[block_rows:], query_stack[...], grad_stack[...], total_row,
+            delta_row, allowed, scale,
+        )
+        query_acc[...] += query_part
+        plane_part[place, slot, :block_rows] = key_part.astype(jnp.bfloat16)
+        plane_part[place, slot, block_rows:] = value_part.astype(jnp.bfloat16)
+    sent += exchange(plane_peer, plane_count, place, lambda p: plane_part.at[place], plane_part, part_send_p, part_recv_p)
+    for head in range(heads):
+        query_grad_ref[:, pl.ds(head * head_width, head_width)] = query_acc[
+            pl.ds(head * block_rows, block_rows), :
+        ]
+    arrive(plane_peer, plane_count, plane_part, part_send_p, part_recv_p)
+
+    sums = jnp.zeros(plane_part.shape[2:], jnp.float32)
+    for offset in range(line_count - 1, -1, -1):
+        peer, _ = line_peer(offset)
+        sums = jnp.zeros(plane_part.shape[2:], jnp.float32)
+        for other in range(plane_count):
+            for slot in range(extra):
+                aimed = plane_info[other, slot][0:1, :] == peer * plane_count + place
+                sums = sums + jnp.where(aimed, plane_part[other, slot].astype(jnp.float32), 0.0)
+        if offset:
+            line_part_out[peer] = sums.astype(jnp.bfloat16)
+    sent += exchange(line_peer, line_count, line, lambda p: line_part_out.at[p], line_part, part_send_l, part_recv_l)
+    key_total = key_acc[...] + sums[:block_rows]
+    value_total = value_acc[...] + sums[block_rows:]
+    arrive(line_peer, line_count, line_part, part_send_l, part_recv_l)
+    for offset in range(1, line_count):
+        peer, _ = line_peer(offset)
+        pair = line_part[peer].astype(jnp.float32)
+        key_total = key_total + pair[:block_rows]
+        value_total = value_total + pair[block_rows:]
+    key_grad_ref[...] = key_total
+    value_grad_ref[...] = value_total
+    for copy in sent:
+        copy.wait_send()
+
+
+def kernel_shards(query_rows, key_rows, value_rows, outputs, out_grads, log_totals, selected, counts):
+    ka_count, pb_count = lax.axis_size("ka"), lax.axis_size("pb")
+    inner = 2 if pb_count % 2 == 0 else 1
+    line_count, plane_count = pb_count // inner, inner * ka_count
+    extra = selected.shape[1] - 1
+    block_rows, head_width = key_rows.shape
+    heads = log_totals.shape[0]
+    pair = (2 * block_rows, head_width)
+    dma = pltpu.SemaphoreType.DMA
+    vmem = pl.BlockSpec(memory_space=pltpu.VMEM)
+    smem = pl.BlockSpec(memory_space=pltpu.SMEM)
+    bf, f32 = jnp.bfloat16, jnp.float32
+    return pl.pallas_call(
+        functools.partial(whole_kernel, ka_count, inner, line_count, extra),
+        out_shape=(
+            jax.ShapeDtypeStruct(query_rows.shape, f32),
+            jax.ShapeDtypeStruct(key_rows.shape, f32),
+            jax.ShapeDtypeStruct(key_rows.shape, f32),
+        ),
+        in_specs=[vmem] * 6 + [smem] * 2,
+        out_specs=(vmem, vmem, vmem),
+        scratch_shapes=[
+            pltpu.VMEM((plane_count, *pair), bf),
+            pltpu.VMEM((line_count, extra, *pair), bf),
+            pltpu.VMEM((line_count, extra, *pair), bf),
+            pltpu.VMEM((plane_count, extra, *pair), bf),
+            pltpu.VMEM((line_count, *pair), bf),
+            pltpu.VMEM((line_count, *pair), bf),
+            pltpu.VMEM((plane_count, extra, 8, 128), jnp.int32),
+            pltpu.VMEM((line_count, extra, 8, 128), jnp.int32),
+            pltpu.VMEM((heads * block_rows, head_width), bf),
+            pltpu.VMEM((heads * block_rows, head_width), bf),
+            pltpu.VMEM((heads * block_rows, head_width), f32),
+            pltpu.VMEM((block_rows, head_width), f32),
+            pltpu.VMEM((block_rows, head_width), f32),
+            *[dma((count,)) for count in (plane_count, plane_count, line_count, line_count) * 3],
+            dma((2,)),
+        ],
+        compiler_params=pltpu.CompilerParams(collective_id=0, has_side_effects=True),
+    )(query_rows, key_rows, value_rows, outputs, out_grads, log_totals, selected, counts)
+
+
+def fits_kernel(query_rows, key_rows, value_rows, outputs, out_grads, log_totals, selected, counts):
+    pb_count, ka_count = lax.axis_size("pb"), lax.axis_size("ka")
+    block_rows, head_width = key_rows.shape
+    inner = 2 if pb_count % 2 == 0 else 1
+    extra = selected.shape[1] - 1
+    tile_bytes = 4 * block_rows * head_width
+    tiles = (pb_count // inner) * (2 * extra + 2) + inner * ka_count * (1 + extra)
+    return (
+        selected.shape[0] == 1
+        and extra > 0
+        and block_rows == head_width == 128
+        and tiles * tile_bytes < VMEM_BUDGET
+    )
+
+
+def either(*arrays):
+    return kernel_shards(*arrays) if fits_kernel(*arrays) else shards(*arrays)
+
+
 def solution(mesh):
     return jax.shard_map(
-        shards,
+        either,
         mesh=mesh,
         in_specs=(
             P(("pb", "ka"), None),

time: 184 us -> 42.1 us (0.23)
  waiting for transfers between devices: 86.5 us -> 0 us
  blocking collectives: 43.3 us -> 0 us
  Pallas kernels: 0 us -> 37.3 us
  between operations: 14.8 us -> 1.3 us
  local copies, waits for them, and re-layouts: 13.8 us -> 3.2 us
  loops' own time: 10.6 us -> 0 us
  other arithmetic: 9.41 us -> 0 us
  starting transfers between devices: 4.04 us -> 0 us
  matrix products: 1.93 us -> 0 us
    reduce_scatter x1 -> x0, waiting for transfers between devices: 66.4 us -> none  [shards(): lax.psum_scatter(key_grads, 'pb', scatter_dimension=0, tiled=True)]
    pallas_call x0 -> x1, Pallas kernels: none -> 37.3 us  [kernel_shards(): pl.pallas_call(functools.partial(whole_kernel, ka_count, inner, line_coun...]
    all_gather x2 -> x0, blocking collectives: 37 us -> none  [the longest x1 31.9 us: shards(): column_keys = lax.all_gather(key_pairs, 'pb', axis=0, tiled=True)]
    ppermute x10 -> x0, waiting for transfers between devices: 20 us -> none  [passed_along(): return lax.ppermute(value, axis, pairs)]
    another operation x5 -> x0, loops' own time: 10.6 us -> none  [the longest x4 10.3 us: visit_block(): return lax.fori_loop(0, live_tiles, one_tile, (query_grad, key_grads))]
    unnamed x1 -> x0, blocking collectives: 6.38 us -> none
    reduce_sum x12 -> x0, other arithmetic: 5.66 us -> none  [the longest x4 5.18 us: visit_block(): live_tiles = jnp.sum(wanted.astype(jnp.int32))]
    ppermute x10 -> x0, starting transfers between devices: 4 us -> none  [passed_along(): return lax.ppermute(value, axis, pairs)]
  transfers between devices with their start and end apart: 11 -> 0, of which waited for: 5 -> 0; matrix products, arithmetic and copies ran while one was open for 7% -> 0% of each run, Pallas kernels for 0% -> 0%
where the time goes in v1:
time: 42.1 us; the launch traced here: 41.8 us
  Pallas kernels  37.3 us (89%)
  local copies, waits for them, and re-layouts  3.2 us (8%)
  between operations  1.3 us (3%)
    pallas_call x1, Pallas kernels, kernel_shards(): pl.pallas_call(functools.partial(whole_kernel, ka_count, inner, line_coun...  37.3 us
    unnamed x7, local copies, waits for them, and re-layouts  3.2 us

profile of v1, /device:TPU:0, one launch (start us, length us, event | category | flops | bytes accessed | tf_op | source)
XLA Modules:
  0.0 41.8 jit_solution(13108127346104905341)
XLA Ops:
  1.3 37.3 %shard_map.103 = (f32[128,512]{1,0:T(8,128)}, f32[128,128]{1,0:T(8,128)}, f32[128,128]{1,0:T(8,128)}) custom-call(bf16[128,512]{1,0:T(8,128)(2,1)} %query_ref.1, bf16[128,128]{1,0:T(8,128)(2,1)} %key_ref.1, bf16[128,128]{1,0:T(8,128)(2,1)} %value_ref.1, bf16[128,512]{1,0:T(8,128)(2,1)} %out_ref.1, bf16[128,512]{1,0:T(8,128)(2,1)} %grad_ref.1, ...), custom_call_target="tpu_custom_call" | custom-call | tf_op jit(solution)/shard_map/pallas_call | solution.py:342
  38.6 0.0 copy-start.1
  38.6 1.7 %copy.15 = f32[128,512]{1,0:T(8,128)} copy(f32[128,512]{1,0:T(8,128)} %get-tuple-element.6) | data formatting | bytes 524288
  40.3 0.0 copy-done.1
  40.4 0.0 copy-start
  40.4 0.6 %copy.16 = f32[128,128]{1,0:T(8,128)} copy(f32[128,128]{1,0:T(8,128)S(1)} %copy-done.1) | data formatting | bytes 131072
  41.0 0.2 copy-done
  41.2 0.6 %copy.17 = f32[128,128]{1,0:T(8,128)} copy(f32[128,128]{1,0:T(8,128)S(1)} %copy-done) | data formatting | bytes 131072
Async XLA Ops:
  38.6 1.7 %copy-start.1 = (f32[128,128]{1,0:T(8,128)S(1)}, f32[128,128]{1,0:T(8,128)}, u32[]{:S(2)}) copy-start(f32[128,128]{1,0:T(8,128)} %get-tuple-element.7) | copy-start | bytes 196612
  40.4 0.9 %copy-start = (f32[128,128]{1,0:T(8,128)S(1)}, f32[128,128]{1,0:T(8,128)}, u32[]{:S(2)}) copy-start(f32[128,128]{1,0:T(8,128)} %get-tuple-element.8) | copy-start | bytes 196612

commit v2 on v0

--- a/solution.py
+++ b/solution.py
@@ -1,6 +1,10 @@
+import functools
+
 import jax
 import jax.numpy as jnp
 from jax import lax
+from jax.experimental import pallas as pl
+from jax.experimental.pallas import tpu as pltpu
 from jax.sharding import PartitionSpec as P
 
 VERY_LOW = -1e30
@@ -138,9 +142,309 @@
     return (query_grad, owned_grads[:, :head_width], owned_grads[:, head_width:])
 
 
+MESH = pl.DeviceIdType.MESH
+VMEM_BUDGET = 40 << 20
+
+
+def tile_weights(key_tile, value_tile, query_stack, grad_stack, total_row, delta_row, allowed, scale):
+    nt = (((1,), (1,)), ((), ()))
+    scores = lax.dot_general(key_tile, query_stack, nt, preferred_element_type=jnp.float32) * scale
+    probs = jnp.exp(jnp.where(allowed, scores - total_row, VERY_LOW))
+    prob_grads = lax.dot_general(value_tile, grad_stack, nt, preferred_element_type=jnp.float32)
+    score_grads = probs * (prob_grads - delta_row)
+    return probs.astype(jnp.bfloat16), score_grads.astype(jnp.bfloat16)
+
+
+def query_share(score_grads, key_tile, scale):
+    tn = (((0,), (0,)), ((), ()))
+    return lax.dot_general(score_grads, key_tile, tn, preferred_element_type=jnp.float32) * scale
+
+
+def whole_kernel(
+    ka_count, inner, line_count, extra,
+    query_hbm, key_hbm, value_hbm, out_hbm, grad_hbm, total_hbm, selected_ref, counts_ref,
+    query_grad_hbm, key_grad_ref, value_grad_ref,
+    query_ref, out_ref, grad_ref, total_ref,
+    key_plane, key_line, key_line_out, value_line, value_plane, value_plane_out,
+    kgrad_plane, kgrad_line, kgrad_line_out, vgrad_line, vgrad_plane, vgrad_plane_out,
+    plane_info, line_info, query_stack, grad_stack, query_acc, key_acc, value_acc,
+    info_send_p, info_recv_p, info_send_l, info_recv_l,
+    key_send_p, key_recv_p, key_send_l, key_recv_l,
+    value_send_p, value_recv_p, value_send_l, value_recv_l,
+    kgrad_send_p, kgrad_recv_p, kgrad_send_l, kgrad_recv_l,
+    vgrad_send_p, vgrad_recv_p, vgrad_send_l, vgrad_recv_l,
+    load_sem,
+):
+    bf, f32 = jnp.bfloat16, jnp.float32
+    plane_count = inner * ka_count
+    pb_index, ka_index = lax.axis_index("pb"), lax.axis_index("ka")
+    line = lax.div(pb_index, inner)
+    row = lax.rem(pb_index, inner)
+    place = row * ka_count + ka_index
+    block_rows, head_width = key_hbm.shape
+    heads = total_hbm.shape[0]
+    scale = head_width ** (-0.5)
+    block = line * plane_count + place
+
+    def plane_peer(offset):
+        peer = lax.rem(place + offset, plane_count)
+        return peer, (line * inner + lax.div(peer, ka_count), lax.rem(peer, ka_count))
+
+    def line_peer(offset):
+        peer = lax.rem(line + offset, line_count)
+        return peer, (peer * inner + row, ka_index)
+
+    plane = (plane_peer, plane_count, place)
+    column = (line_peer, line_count, line)
+
+    barrier = pltpu.get_barrier_semaphore()
+    for peer_of, count, _ in (plane, column):
+        for offset in range(1, count):
+            pl.semaphore_signal(barrier, inc=1, device_id=peer_of(offset)[1], device_id_type=MESH)
+    loads = [
+        pltpu.make_async_copy(source, target, load_sem.at[index])
+        for index, (source, target) in enumerate((
+            (key_hbm, key_plane.at[place]), (value_hbm, value_line.at[line]),
+            (query_hbm, query_ref), (grad_hbm, grad_ref), (out_hbm, out_ref), (total_hbm, total_ref),
+        ))
+    ]
+    for load in loads:
+        load.start()
+
+    targets = [
+        jnp.where(slot + 1 < counts_ref[0], selected_ref[0, slot + 1], -1) for slot in range(extra)
+    ]
+    for slot in range(extra):
+        lines = jnp.full((8, 128), targets[slot], jnp.int32)
+        plane_info[place, slot] = lines
+        line_info[line, slot] = lines
+
+    sent = []
+
+    def send(group, offset, source, target, send_sem, recv_sem):
+        peer_of, _, me = group
+        copy = pltpu.make_async_remote_copy(
+            src_ref=source, dst_ref=target.at[me], send_sem=send_sem.at[offset],
+            recv_sem=recv_sem.at[me], device_id=peer_of(offset)[1], device_id_type=MESH,
+        )
+        copy.start()
+        sent.append(copy)
+
+    def spread(group, target, send_sem, recv_sem):
+        for offset in range(1, group[1]):
+            send(group, offset, target.at[group[2]], target, send_sem, recv_sem)
+
+    def arrive(group, target, send_sem, recv_sem):
+        peer_of, count, _ = group
+        for offset in range(1, count):
+            peer, device = peer_of(offset)
+            pltpu.make_async_remote_copy(
+                src_ref=target.at[peer], dst_ref=target.at[peer], send_sem=send_sem.at[offset],
+                recv_sem=recv_sem.at[peer], device_id=device, device_id_type=MESH,
+            ).wait_recv()
+
+    loads[0].wait()
+    loads[1].wait()
+    pl.semaphore_wait(barrier, plane_count + line_count - 2)
+    spread(column, line_info, info_send_l, info_recv_l)
+    spread(plane, plane_info, info_send_p, info_recv_p)
+    spread(column, value_line, value_send_l, value_recv_l)
+    spread(plane, key_plane, key_send_p, key_recv_p)
+
+    for load in loads[2:]:
+        load.wait()
+    deltas = []
+    for head in range(heads):
+        columns = pl.ds(head * head_width, head_width)
+        rows = pl.ds(head * block_rows, block_rows)
+        query_stack[rows, :] = query_ref[:, columns]
+        grad_stack[rows, :] = grad_ref[:, columns]
+        product = grad_ref[:, columns].astype(f32) * out_ref[:, columns].astype(f32)
+        deltas.append(jnp.sum(product.T, axis=0, keepdims=True))
+    delta_row = jnp.concatenate(deltas, axis=1)
+    total_row = jnp.concatenate([total_ref[head : head + 1, :] for head in range(heads)], axis=1)
+    stack_shape = (block_rows, heads * block_rows)
+    key_offset = lax.broadcasted_iota(jnp.int32, stack_shape, 0)
+    query_offset = lax.rem(lax.broadcasted_iota(jnp.int32, stack_shape, 1), block_rows)
+
+    arrive(column, line_info, info_send_l, info_recv_l)
+    arrive(plane, plane_info, info_send_p, info_recv_p)
+
+    def pick(group, info, held, held_count, first, step, out, target, send_sem, recv_sem):
+        peer_of, count, me = group
+        for offset in list(range(1, count)) + [0]:
+            peer, _ = peer_of(offset)
+            for slot in range(extra):
+                wanted = info[peer, slot][0:1, :]
+                picked = jnp.zeros(held.shape[1:], f32)
+                for other in range(held_count):
+                    picked = jnp.where(wanted == first + other * step, held[other].astype(f32), picked)
+                if offset:
+                    out[peer, slot] = picked.astype(bf)
+                else:
+                    target[me, slot] = picked.astype(bf)
+            if offset:
+                send(group, offset, out.at[peer], target, send_sem, recv_sem)
+
+    arrive(column, value_line, value_send_l, value_recv_l)
+    pick(plane, plane_info, value_line, line_count, place, plane_count,
+         value_plane_out, value_plane, value_send_p, value_recv_p)
+    arrive(plane, key_plane, key_send_p, key_recv_p)
+    pick(column, line_info, key_plane, plane_count, line * plane_count, 1,
+         key_line_out, key_line, key_send_l, key_recv_l)
+
+    own_key = key_plane[place]
+    probs, score_grads = tile_weights(
+        own_key, value_line[line], query_stack[...], grad_stack[...], total_row, delta_row,
+        key_offset <= query_offset, scale,
+    )
+    query_acc[...] = query_share(score_grads, own_key, scale)
+    key_acc[...] = jnp.dot(score_grads, query_stack[...], preferred_element_type=f32) * scale
+    value_acc[...] = jnp.dot(probs, grad_stack[...], preferred_element_type=f32)
+
+    arrive(column, key_line, key_send_l, key_recv_l)
+    arrive(plane, value_plane, value_send_p, value_recv_p)
+    late = []
+    for slot in range(extra):
+        listed = jnp.maximum(targets[slot], 0)
+        key_tile = key_line[lax.div(listed, plane_count), slot]
+        value_tile = value_plane[lax.rem(listed, plane_count), slot]
+        allowed = (key_offset + targets[slot] * block_rows <= query_offset + block * block_rows) & (
+            jnp.full(stack_shape, targets[slot], jnp.int32) >= 0
+        )
+        probs, score_grads = tile_weights(
+            key_tile, value_tile, query_stack[...], grad_stack[...], total_row, delta_row, allowed, scale
+        )
+        vgrad_line[line, slot] = jnp.dot(probs, grad_stack[...], preferred_element_type=f32).astype(bf)
+        kgrad_plane[place, slot] = (
+            jnp.dot(score_grads, query_stack[...], preferred_element_type=f32) * scale
+        ).astype(bf)
+        late.append((score_grads, key_tile))
+    spread(column, vgrad_line, vgrad_send_l, vgrad_recv_l)
+    spread(plane, kgrad_plane, kgrad_send_p, kgrad_recv_p)
+    for score_grads, key_tile in late:
+        query_acc[...] += query_share(score_grads, key_tile, scale)
+    stores = []
+    for head in range(heads):
+        store = pltpu.make_async_copy(
+            query_acc.at[pl.ds(head * block_rows, block_rows), :],
+            query_grad_hbm.at[:, pl.ds(head * head_width, head_width)],
+            load_sem.at[len(loads) + head],
+        )
+        store.start()
+        stores.append(store)
+
+    def combine(group, info, held, held_count, first, step, out, target, send_sem, recv_sem):
+        peer_of, count, _ = group
+        for offset in list(range(1, count)) + [0]:
+            peer, _ = peer_of(offset)
+            sums = jnp.zeros(held.shape[2:], f32)
+            for other in range(held_count):
+                for slot in range(extra):
+                    aimed = info[other, slot][0:1, :] == first + peer * step
+                    sums = sums + jnp.where(aimed, held[other, slot].astype(f32), 0.0)
+            if offset:
+                out[peer] = sums.astype(bf)
+                send(group, offset, out.at[peer], target, send_sem, recv_sem)
+        return sums
+
+    arrive(column, vgrad_line, vgrad_send_l, vgrad_recv_l)
+    value_total = combine(plane, line_info, vgrad_line, line_count, line * plane_count, 1,
+                          vgrad_plane_out, vgrad_plane, vgrad_send_p, vgrad_recv_p)
+    arrive(plane, kgrad_plane, kgrad_send_p, kgrad_recv_p)
+    key_total = combine(column, plane_info, kgrad_plane, plane_count, place, plane_count,
+                        kgrad_line_out, kgrad_line, kgrad_send_l, kgrad_recv_l)
+    value_total = value_total + value_acc[...]
+    key_total = key_total + key_acc[...]
+    arrive(column, kgrad_line, kgrad_send_l, kgrad_recv_l)
+    for offset in range(1, line_count):
+        key_total = key_total + kgrad_line[line_peer(offset)[0]].astype(f32)
+    key_grad_ref[...] = key_total
+    arrive(plane, vgrad_plane, vgrad_send_p, vgrad_recv_p)
+    for offset in range(1, plane_count):
+        value_total = value_total + vgrad_plane[plane_peer(offset)[0]].astype(f32)
+    value_grad_ref[...] = value_total
+    for copy in sent:
+        copy.wait_send()
+    for store in stores:
+        store.wait()
+
+
+def kernel_shards(query_rows, key_rows, value_rows, outputs, out_grads, log_totals, selected, counts):
+    ka_count, pb_count = lax.axis_size("ka"), lax.axis_size("pb")
+    inner = 2 if pb_count % 2 == 0 else 1
+    line_count, plane_count = pb_count // inner, inner * ka_count
+    extra = selected.shape[1] - 1
+    block_rows, head_width = key_rows.shape
+    heads = log_totals.shape[0]
+    tile = key_rows.shape
+    dma = pltpu.SemaphoreType.DMA
+    vmem = pl.BlockSpec(memory_space=pltpu.VMEM)
+    smem = pl.BlockSpec(memory_space=pltpu.SMEM)
+    hbm = pl.BlockSpec(memory_space=pl.ANY)
+    bf, f32 = jnp.bfloat16, jnp.float32
+    return pl.pallas_call(
+        functools.partial(whole_kernel, ka_count, inner, line_count, extra),
+        out_shape=(
+            jax.ShapeDtypeStruct(query_rows.shape, f32),
+            jax.ShapeDtypeStruct(key_rows.shape, f32),
+            jax.ShapeDtypeStruct(key_rows.shape, f32),
+        ),
+        in_specs=[hbm] * 6 + [smem] * 2,
+        out_specs=(hbm, vmem, vmem),
+        scratch_shapes=[
+            pltpu.VMEM(query_rows.shape, bf),
+            pltpu.VMEM(query_rows.shape, bf),
+            pltpu.VMEM(query_rows.shape, bf),
+            pltpu.VMEM(log_totals.shape, f32),
+            pltpu.VMEM((plane_count, *tile), bf),
+            pltpu.VMEM((line_count, extra, *tile), bf),
+            pltpu.VMEM((line_count, extra, *tile), bf),
+            pltpu.VMEM((line_count, *tile), bf),
+            pltpu.VMEM((plane_count, extra, *tile), bf),
+            pltpu.VMEM((plane_count, extra, *tile), bf),
+            pltpu.VMEM((plane_count, extra, *tile), bf),
+            pltpu.VMEM((line_count, *tile), bf),
+            pltpu.VMEM((line_count, *tile), bf),
+            pltpu.VMEM((line_count, extra, *tile), bf),
+            pltpu.VMEM((plane_count, *tile), bf),
+            pltpu.VMEM((plane_count, *tile), bf),
+            pltpu.VMEM((plane_count, extra, 8, 128), jnp.int32),
+            pltpu.VMEM((line_count, extra, 8, 128), jnp.int32),
+            pltpu.VMEM((heads * block_rows, head_width), bf),
+            pltpu.VMEM((heads * block_rows, head_width), bf),
+            pltpu.VMEM((heads * block_rows, head_width), f32),
+            pltpu.VMEM(tile, f32),
+            pltpu.VMEM(tile, f32),
+            *[dma((count,)) for count in (plane_count, plane_count, line_count, line_count) * 5],
+            dma((6 + heads,)),
+        ],
+        compiler_params=pltpu.CompilerParams(collective_id=0, has_side_effects=True),
+    )(query_rows, key_rows, value_rows, outputs, out_grads, log_totals, selected, counts)
+
+
+def fits_kernel(query_rows, key_rows, value_rows, outputs, out_grads, log_totals, selected, counts):
+    pb_count, ka_count = lax.axis_size("pb"), lax.axis_size("ka")
+    block_rows, head_width = key_rows.shape
+    inner = 2 if pb_count % 2 == 0 else 1
+    extra = selected.shape[1] - 1
+    tile_bytes = 2 * block_rows * head_width
+    tiles = 3 * (pb_count // inner + inner * ka_count) * (1 + extra)
+    return (
+        selected.shape[0] == 1
+        and extra > 0
+        and block_rows == head_width == 128
+        and tiles * tile_bytes < VMEM_BUDGET
+    )
+
+
+def either(*arrays):
+    return kernel_shards(*arrays) if fits_kernel(*arrays) else shards(*arrays)
+
+
 def solution(mesh):
     return jax.shard_map(
-        shards,
+        either,
         mesh=mesh,
         in_specs=(
             P(("pb", "ka"), None),

time: 184 us -> 32 us (0.17)
  waiting for transfers between devices: 86.5 us -> 0 us
  blocking collectives: 43.3 us -> 0 us
  Pallas kernels: 0 us -> 27.3 us
  between operations: 14.8 us -> 1.3 us
  local copies, waits for them, and re-layouts: 13.8 us -> 3.2 us
  loops' own time: 10.6 us -> 0 us
  other arithmetic: 9.41 us -> 0 us
  starting transfers between devices: 4.04 us -> 0 us
  matrix products: 1.93 us -> 0 us
    reduce_scatter x1 -> x0, waiting for transfers between devices: 66.4 us -> none  [shards(): lax.psum_scatter(key_grads, 'pb', scatter_dimension=0, tiled=True)]
    all_gather x2 -> x0, blocking collectives: 37 us -> none  [the longest x1 31.9 us: shards(): column_keys = lax.all_gather(key_pairs, 'pb', axis=0, tiled=True)]
    pallas_call x0 -> x1, Pallas kernels: none -> 27.3 us  [kernel_shards(): pl.pallas_call(functools.partial(whole_kernel, ka_count, inner, line_coun...]
    ppermute x10 -> x0, waiting for transfers between devices: 20 us -> none  [passed_along(): return lax.ppermute(value, axis, pairs)]
    another operation x5 -> x0, loops' own time: 10.6 us -> none  [the longest x4 10.3 us: visit_block(): return lax.fori_loop(0, live_tiles, one_tile, (query_grad, key_grads))]
    unnamed x1 -> x0, blocking collectives: 6.38 us -> none
    reduce_sum x12 -> x0, other arithmetic: 5.66 us -> none  [the longest x4 5.18 us: visit_block(): live_tiles = jnp.sum(wanted.astype(jnp.int32))]
    ppermute x10 -> x0, starting transfers between devices: 4 us -> none  [passed_along(): return lax.ppermute(value, axis, pairs)]
  transfers between devices with their start and end apart: 11 -> 0, of which waited for: 5 -> 0; matrix products, arithmetic and copies ran while one was open for 7% -> 0% of each run, Pallas kernels for 0% -> 0%
where the time goes in v2:
time: 32 us; the launch traced here: 31.7 us
  Pallas kernels  27.3 us (85%)
  local copies, waits for them, and re-layouts  3.2 us (10%)
  between operations  1.3 us (4%)
    pallas_call x1, Pallas kernels, kernel_shards(): pl.pallas_call(functools.partial(whole_kernel, ka_count, inner, line_coun...  27.3 us
    unnamed x7, local copies, waits for them, and re-layouts  3.2 us

profile of v2, /device:TPU:0, one launch (start us, length us, event | category | flops | bytes accessed | tf_op | source)
XLA Modules:
  0.0 31.7 jit_solution(10792126790898108228)
XLA Ops:
  1.3 27.3 %shard_map.103 = (f32[128,512]{1,0:T(8,128)}, f32[128,128]{1,0:T(8,128)}, f32[128,128]{1,0:T(8,128)}) custom-call(bf16[128,512]{1,0:T(8,128)(2,1)} %query_hbm.1, bf16[128,128]{1,0:T(8,128)(2,1)} %key_hbm.1, bf16[128,128]{1,0:T(8,128)(2,1)} %value_hbm.1, bf16[128,512]{1,0:T(8,128)(2,1)} %out_hbm.1, bf16[128,512]{1,0:T(8,128)(2,1)} %grad_hbm.1, ...), custom_call_target="tpu_custom_call" | custom-call | tf_op jit(solution)/shard_map/pallas_call | solution.py:386
  28.5 0.0 copy-start.1
  28.6 1.7 %copy.15 = f32[128,512]{1,0:T(8,128)} copy(f32[128,512]{1,0:T(8,128)} %get-tuple-element.6) | data formatting | bytes 524288
  30.3 0.0 copy-done.1
  30.3 0.0 copy-start
  30.3 0.6 %copy.16 = f32[128,128]{1,0:T(8,128)} copy(f32[128,128]{1,0:T(8,128)S(1)} %copy-done.1) | data formatting | bytes 131072
  30.9 0.2 copy-done
  31.1 0.6 %copy.17 = f32[128,128]{1,0:T(8,128)} copy(f32[128,128]{1,0:T(8,128)S(1)} %copy-done) | data formatting | bytes 131072
Async XLA Ops:
  28.5 1.7 %copy-start.1 = (f32[128,128]{1,0:T(8,128)S(1)}, f32[128,128]{1,0:T(8,128)}, u32[]{:S(2)}) copy-start(f32[128,128]{1,0:T(8,128)} %get-tuple-element.7) | copy-start | bytes 196612
  30.3 0.9 %copy-start = (f32[128,128]{1,0:T(8,128)S(1)}, f32[128,128]{1,0:T(8,128)}, u32[]{:S(2)}) copy-start(f32[128,128]{1,0:T(8,128)} %get-tuple-element.8) | copy-start | bytes 196612

commit v3 on v2

--- a/solution.py
+++ b/solution.py
@@ -163,7 +163,7 @@
 def whole_kernel(
     ka_count, inner, line_count, extra,
     query_hbm, key_hbm, value_hbm, out_hbm, grad_hbm, total_hbm, selected_ref, counts_ref,
-    query_grad_hbm, key_grad_ref, value_grad_ref,
+    query_grad_ref, key_grad_ref, value_grad_ref,
     query_ref, out_ref, grad_ref, total_ref,
     key_plane, key_line, key_line_out, value_line, value_plane, value_plane_out,
     kgrad_plane, kgrad_line, kgrad_line_out, vgrad_line, vgrad_plane, vgrad_plane_out,
@@ -324,15 +324,10 @@
     spread(plane, kgrad_plane, kgrad_send_p, kgrad_recv_p)
     for score_grads, key_tile in late:
         query_acc[...] += query_share(score_grads, key_tile, scale)
-    stores = []
     for head in range(heads):
-        store = pltpu.make_async_copy(
-            query_acc.at[pl.ds(head * block_rows, block_rows), :],
-            query_grad_hbm.at[:, pl.ds(head * head_width, head_width)],
-            load_sem.at[len(loads) + head],
-        )
-        store.start()
-        stores.append(store)
+        query_grad_ref[:, pl.ds(head * head_width, head_width)] = query_acc[
+            pl.ds(head * block_rows, block_rows), :
+        ]
 
     def combine(group, info, held, held_count, first, step, out, target, send_sem, recv_sem):
         peer_of, count, _ = group
@@ -366,8 +361,6 @@
     value_grad_ref[...] = value_total
     for copy in sent:
         copy.wait_send()
-    for store in stores:
-        store.wait()
 
 
 def kernel_shards(query_rows, key_rows, value_rows, outputs, out_grads, log_totals, selected, counts):
@@ -383,15 +376,12 @@
     smem = pl.BlockSpec(memory_space=pltpu.SMEM)
     hbm = pl.BlockSpec(memory_space=pl.ANY)
     bf, f32 = jnp.bfloat16, jnp.float32
-    return pl.pallas_call(
+    shapes = (query_rows.shape, key_rows.shape, value_rows.shape)
+    held = pl.pallas_call(
         functools.partial(whole_kernel, ka_count, inner, line_count, extra),
-        out_shape=(
-            jax.ShapeDtypeStruct(query_rows.shape, f32),
-            jax.ShapeDtypeStruct(key_rows.shape, f32),
-            jax.ShapeDtypeStruct(key_rows.shape, f32),
-        ),
+        out_shape=tuple(pltpu.VMEM(shape, f32) for shape in shapes),
         in_specs=[hbm] * 6 + [smem] * 2,
-        out_specs=(hbm, vmem, vmem),
+        out_specs=(vmem, vmem, vmem),
         scratch_shapes=[
             pltpu.VMEM(query_rows.shape, bf),
             pltpu.VMEM(query_rows.shape, bf),
@@ -417,10 +407,26 @@
             pltpu.VMEM(tile, f32),
             pltpu.VMEM(tile, f32),
             *[dma((count,)) for count in (plane_count, plane_count, line_count, line_count) * 5],
-            dma((6 + heads,)),
+            dma((6,)),
         ],
         compiler_params=pltpu.CompilerParams(collective_id=0, has_side_effects=True),
     )(query_rows, key_rows, value_rows, outputs, out_grads, log_totals, selected, counts)
+    return pl.pallas_call(
+        write_kernel,
+        out_shape=tuple(jax.ShapeDtypeStruct(shape, f32) for shape in shapes),
+        in_specs=[vmem] * 3,
+        out_specs=(hbm, hbm, hbm),
+        scratch_shapes=[dma((3,))],
+    )(*[pltpu.with_memory_space_constraint(part, pltpu.VMEM) for part in held])
+
+
+def write_kernel(*refs):
+    sources, targets, sem = refs[:3], refs[3:6], refs[6]
+    stores = [pltpu.make_async_copy(*pair, sem.at[i]) for i, pair in enumerate(zip(sources, targets))]
+    for store in stores:
+        store.start()
+    for store in stores:
+        store.wait()
 
 
 def fits_kernel(query_rows, key_rows, value_rows, outputs, out_grads, log_totals, selected, counts):

time: 32 us -> 28.8 us (0.900)
  local copies, waits for them, and re-layouts: 3.2 us -> 0 us
    unnamed x7 -> x0, local copies, waits for them, and re-layouts: 3.2 us -> none
    pallas_call x0 -> x1, Pallas kernels: none -> 0.77 us  [kernel_shards(): pl.pallas_call(write_kernel, out_shape=tuple((jax.ShapeDtypeStruct(shape,...]
    pallas_call x1, Pallas kernels: 27.3 us -> 26.5 us  [kernel_shards(): pl.pallas_call(functools.partial(whole_kernel, ka_count, inner, line_coun...]
where the time goes in v3:
time: 28.8 us; the launch traced here: 28.6 us
  Pallas kernels  27.3 us (95%)
  between operations  1.29 us (4%)
    pallas_call x1, Pallas kernels, kernel_shards(): pl.pallas_call(functools.partial(whole_kernel, ka_count, inner, line_coun...  26.5 us
    pallas_call x1, Pallas kernels, kernel_shards(): pl.pallas_call(write_kernel, out_shape=tuple((jax.ShapeDtypeStruct(shape,...  0.77 us

profile of v3, /device:TPU:0, one launch (start us, length us, event | category | flops | bytes accessed | tf_op | source)
XLA Modules:
  0.0 28.6 jit_solution(642564657156020638)
XLA Ops:
  1.3 26.5 %shard_map.103 = (f32[128,512]{1,0:T(8,128)S(1)}, f32[128,128]{1,0:T(8,128)S(1)}, f32[128,128]{1,0:T(8,128)S(1)}) custom-call(bf16[128,512]{1,0:T(8,128)(2,1)} %query_hbm.1, bf16[128,128]{1,0:T(8,128)(2,1)} %key_hbm.1, bf16[128,128]{1,0:T(8,128)(2,1)} %value_hbm.1, bf16[128,512]{1,0:T(8,128)(2,1)} %out_hbm.1, bf16[128,512]{1,0:T(8,128)(2,1)} %grad_hbm.1, ...), custom_call_target="tpu_custom_call" | custom-call | tf_op jit(solution)/shard_map/pallas_call | solution.py:380
  27.8 0.8 %shard_map.104 = (f32[128,512]{1,0:T(8,128)}, f32[128,128]{1,0:T(8,128)}, f32[128,128]{1,0:T(8,128)}) custom-call(f32[128,512]{1,0:T(8,128)S(1)} %get-tuple-element.6.refs_0_, f32[128,128]{1,0:T(8,128)S(1)} %get-tuple-element.7.refs_1_, f32[128,128]{1,0:T(8,128)S(1)} %get-tuple-element.8.refs_2_), custom_call_target="tpu_custom_call" | custom-call | tf_op jit(solution)/shard_map/pallas_call | solution.py:414

commit v4 on v3

--- a/solution.py
+++ b/solution.py
@@ -161,7 +161,7 @@
 
 
 def whole_kernel(
-    ka_count, inner, line_count, extra,
+    ka_count, inner, line_count, extra, chunks,
     query_hbm, key_hbm, value_hbm, out_hbm, grad_hbm, total_hbm, selected_ref, counts_ref,
     query_grad_ref, key_grad_ref, value_grad_ref,
     query_ref, out_ref, grad_ref, total_ref,
@@ -184,6 +184,8 @@
     block_rows, head_width = key_hbm.shape
     heads = total_hbm.shape[0]
     scale = head_width ** (-0.5)
+    chunk_rows = block_rows // chunks
+    spans = [pl.ds(chunk * chunk_rows, chunk_rows) for chunk in range(chunks)]
     block = line * plane_count + place
 
     def plane_peer(offset):
@@ -201,12 +203,13 @@
     for peer_of, count, _ in (plane, column):
         for offset in range(1, count):
             pl.semaphore_signal(barrier, inc=1, device_id=peer_of(offset)[1], device_id_type=MESH)
+    moves = []
+    for chunk, span in enumerate(spans):
+        moves.append((key_hbm.at[span], key_plane.at[place, chunk]))
+        moves.append((value_hbm.at[span], value_line.at[line, chunk]))
+    moves += [(query_hbm, query_ref), (grad_hbm, grad_ref), (out_hbm, out_ref), (total_hbm, total_ref)]
     loads = [
-        pltpu.make_async_copy(source, target, load_sem.at[index])
-        for index, (source, target) in enumerate((
-            (key_hbm, key_plane.at[place]), (value_hbm, value_line.at[line]),
-            (query_hbm, query_ref), (grad_hbm, grad_ref), (out_hbm, out_ref), (total_hbm, total_ref),
-        ))
+        pltpu.make_async_copy(*move, load_sem.at[index]) for index, move in enumerate(moves)
     ]
     for load in loads:
         load.start()
@@ -216,42 +219,44 @@
     ]
     for slot in range(extra):
         lines = jnp.full((8, 128), targets[slot], jnp.int32)
-        plane_info[place, slot] = lines
-        line_info[line, slot] = lines
+        plane_info[place, 0, slot] = lines
+        line_info[line, 0, slot] = lines
 
     sent = []
 
-    def send(group, offset, source, target, send_sem, recv_sem):
+    def send(group, offset, chunk, source, target, send_sem, recv_sem):
         peer_of, _, me = group
         copy = pltpu.make_async_remote_copy(
-            src_ref=source, dst_ref=target.at[me], send_sem=send_sem.at[offset],
-            recv_sem=recv_sem.at[me], device_id=peer_of(offset)[1], device_id_type=MESH,
+            src_ref=source, dst_ref=target.at[me, chunk], send_sem=send_sem.at[offset, chunk],
+            recv_sem=recv_sem.at[me, chunk], device_id=peer_of(offset)[1], device_id_type=MESH,
         )
         copy.start()
         sent.append(copy)
 
-    def spread(group, target, send_sem, recv_sem):
+    def spread(group, chunk, target, send_sem, recv_sem):
         for offset in range(1, group[1]):
-            send(group, offset, target.at[group[2]], target, send_sem, recv_sem)
-
-    def arrive(group, target, send_sem, recv_sem):
+            send(group, offset, chunk, target.at[group[2], chunk], target, send_sem, recv_sem)
+
+    def arrive(group, chunk, target, send_sem, recv_sem):
         peer_of, count, _ = group
         for offset in range(1, count):
             peer, device = peer_of(offset)
             pltpu.make_async_remote_copy(
-                src_ref=target.at[peer], dst_ref=target.at[peer], send_sem=send_sem.at[offset],
-                recv_sem=recv_sem.at[peer], device_id=device, device_id_type=MESH,
+                src_ref=target.at[peer, chunk], dst_ref=target.at[peer, chunk],
+                send_sem=send_sem.at[offset, chunk], recv_sem=recv_sem.at[peer, chunk],
+                device_id=device, device_id_type=MESH,
             ).wait_recv()
 
-    loads[0].wait()
-    loads[1].wait()
+    for load in loads[: 2 * chunks]:
+        load.wait()
     pl.semaphore_wait(barrier, plane_count + line_count - 2)
-    spread(column, line_info, info_send_l, info_recv_l)
-    spread(plane, plane_info, info_send_p, info_recv_p)
-    spread(column, value_line, value_send_l, value_recv_l)
-    spread(plane, key_plane, key_send_p, key_recv_p)
-
-    for load in loads[2:]:
+    spread(column, 0, line_info, info_send_l, info_recv_l)
+    spread(plane, 0, plane_info, info_send_p, info_recv_p)
+    for chunk in range(chunks):
+        spread(column, chunk, value_line, value_send_l, value_recv_l)
+        spread(plane, chunk, key_plane, key_send_p, key_recv_p)
+
+    for load in loads[2 * chunks :]:
         load.wait()
     deltas = []
     for head in range(heads):
@@ -267,61 +272,73 @@
     key_offset = lax.broadcasted_iota(jnp.int32, stack_shape, 0)
     query_offset = lax.rem(lax.broadcasted_iota(jnp.int32, stack_shape, 1), block_rows)
 
-    arrive(column, line_info, info_send_l, info_recv_l)
-    arrive(plane, plane_info, info_send_p, info_recv_p)
-
-    def pick(group, info, held, held_count, first, step, out, target, send_sem, recv_sem):
+    arrive(column, 0, line_info, info_send_l, info_recv_l)
+    arrive(plane, 0, plane_info, info_send_p, info_recv_p)
+
+    def pick(group, chunk, info, held, held_count, first, step, out, target, send_sem, recv_sem):
         peer_of, count, me = group
         for offset in list(range(1, count)) + [0]:
             peer, _ = peer_of(offset)
             for slot in range(extra):
-                wanted = info[peer, slot][0:1, :]
-                picked = jnp.zeros(held.shape[1:], f32)
+                wanted = info[peer, 0, slot][0:1, :]
+                picked = jnp.zeros(held.shape[2:], f32)
                 for other in range(held_count):
-                    picked = jnp.where(wanted == first + other * step, held[other].astype(f32), picked)
+                    picked = jnp.where(
+                        wanted == first + other * step, held[other, chunk].astype(f32), picked
+                    )
                 if offset:
-                    out[peer, slot] = picked.astype(bf)
+                    out[peer, chunk, slot] = picked.astype(bf)
                 else:
-                    target[me, slot] = picked.astype(bf)
+                    target[me, chunk, slot] = picked.astype(bf)
             if offset:
-                send(group, offset, out.at[peer], target, send_sem, recv_sem)
-
-    arrive(column, value_line, value_send_l, value_recv_l)
-    pick(plane, plane_info, value_line, line_count, place, plane_count,
-         value_plane_out, value_plane, value_send_p, value_recv_p)
-    arrive(plane, key_plane, key_send_p, key_recv_p)
-    pick(column, line_info, key_plane, plane_count, line * plane_count, 1,
-         key_line_out, key_line, key_send_l, key_recv_l)
-
-    own_key = key_plane[place]
+                send(group, offset, chunk, out.at[peer, chunk], target, send_sem, recv_sem)
+
+    for chunk in range(chunks):
+        arrive(column, chunk, value_line, value_send_l, value_recv_l)
+        pick(plane, chunk, plane_info, value_line, line_count, place, plane_count,
+             value_plane_out, value_plane, value_send_p, value_recv_p)
+        arrive(plane, chunk, key_plane, key_send_p, key_recv_p)
+        pick(column, chunk, line_info, key_plane, plane_count, line * plane_count, 1,
+             key_line_out, key_line, key_send_l, key_recv_l)
+
+    def whole(parts):
+        return jnp.concatenate(parts, axis=0)
+
+    own_key = whole([key_plane[place, chunk] for chunk in range(chunks)])
+    own_value = whole([value_line[line, chunk] for chunk in range(chunks)])
     probs, score_grads = tile_weights(
-        own_key, value_line[line], query_stack[...], grad_stack[...], total_row, delta_row,
+        own_key, own_value, query_stack[...], grad_stack[...], total_row, delta_row,
         key_offset <= query_offset, scale,
     )
     query_acc[...] = query_share(score_grads, own_key, scale)
     key_acc[...] = jnp.dot(score_grads, query_stack[...], preferred_element_type=f32) * scale
     value_acc[...] = jnp.dot(probs, grad_stack[...], preferred_element_type=f32)
 
-    arrive(column, key_line, key_send_l, key_recv_l)
-    arrive(plane, value_plane, value_send_p, value_recv_p)
+    for chunk in range(chunks):
+        arrive(column, chunk, key_line, key_send_l, key_recv_l)
+        arrive(plane, chunk, value_plane, value_send_p, value_recv_p)
     late = []
     for slot in range(extra):
         listed = jnp.maximum(targets[slot], 0)
-        key_tile = key_line[lax.div(listed, plane_count), slot]
-        value_tile = value_plane[lax.rem(listed, plane_count), slot]
+        source, spot = lax.div(listed, plane_count), lax.rem(listed, plane_count)
+        key_tile = whole([key_line[source, chunk, slot] for chunk in range(chunks)])
+        value_tile = whole([value_plane[spot, chunk, slot] for chunk in range(chunks)])
         allowed = (key_offset + targets[slot] * block_rows <= query_offset + block * block_rows) & (
             jnp.full(stack_shape, targets[slot], jnp.int32) >= 0
         )
         probs, score_grads = tile_weights(
             key_tile, value_tile, query_stack[...], grad_stack[...], total_row, delta_row, allowed, scale
         )
-        vgrad_line[line, slot] = jnp.dot(probs, grad_stack[...], preferred_element_type=f32).astype(bf)
-        kgrad_plane[place, slot] = (
-            jnp.dot(score_grads, query_stack[...], preferred_element_type=f32) * scale
-        ).astype(bf)
+        value_part = jnp.dot(probs, grad_stack[...], preferred_element_type=f32).astype(bf)
+        key_part = (jnp.dot(score_grads, query_stack[...], preferred_element_type=f32) * scale).astype(bf)
+        for chunk in range(chunks):
+            rows = slice(chunk * chunk_rows, (chunk + 1) * chunk_rows)
+            vgrad_line[line, chunk, slot] = value_part[rows]
+            kgrad_plane[place, chunk, slot] = key_part[rows]
         late.append((score_grads, key_tile))
-    spread(column, vgrad_line, vgrad_send_l, vgrad_recv_l)
-    spread(plane, kgrad_plane, kgrad_send_p, kgrad_recv_p)
+    for chunk in range(chunks):
+        spread(column, chunk, vgrad_line, vgrad_send_l, vgrad_recv_l)
+        spread(plane, chunk, kgrad_plane, kgrad_send_p, kgrad_recv_p)
     for score_grads, key_tile in late:
         query_acc[...] += query_share(score_grads, key_tile, scale)
     for head in range(heads):
@@ -329,36 +346,40 @@
             pl.ds(head * block_rows, block_rows), :
         ]
 
-    def combine(group, info, held, held_count, first, step, out, target, send_sem, recv_sem):
+    def combine(group, chunk, info, held, held_count, first, step, out, target, send_sem, recv_sem):
         peer_of, count, _ = group
         for offset in list(range(1, count)) + [0]:
             peer, _ = peer_of(offset)
-            sums = jnp.zeros(held.shape[2:], f32)
+            sums = jnp.zeros(held.shape[3:], f32)
             for other in range(held_count):
                 for slot in range(extra):
-                    aimed = info[other, slot][0:1, :] == first + peer * step
-                    sums = sums + jnp.where(aimed, held[other, slot].astype(f32), 0.0)
+                    aimed = info[other, 0, slot][0:1, :] == first + peer * step
+                    sums = sums + jnp.where(aimed, held[other, chunk, slot].astype(f32), 0.0)
             if offset:
-                out[peer] = sums.astype(bf)
-                send(group, offset, out.at[peer], target, send_sem, recv_sem)
+                out[peer, chunk] = sums.astype(bf)
+                send(group, offset, chunk, out.at[peer, chunk], target, send_sem, recv_sem)
         return sums
 
-    arrive(column, vgrad_line, vgrad_send_l, vgrad_recv_l)
-    value_total = combine(plane, line_info, vgrad_line, line_count, line * plane_count, 1,
-                          vgrad_plane_out, vgrad_plane, vgrad_send_p, vgrad_recv_p)
-    arrive(plane, kgrad_plane, kgrad_send_p, kgrad_recv_p)
-    key_total = combine(column, plane_info, kgrad_plane, plane_count, place, plane_count,
-                        kgrad_line_out, kgrad_line, kgrad_send_l, kgrad_recv_l)
-    value_total = value_total + value_acc[...]
-    key_total = key_total + key_acc[...]
-    arrive(column, kgrad_line, kgrad_send_l, kgrad_recv_l)
-    for offset in range(1, line_count):
-        key_total = key_total + kgrad_line[line_peer(offset)[0]].astype(f32)
-    key_grad_ref[...] = key_total
-    arrive(plane, vgrad_plane, vgrad_send_p, vgrad_recv_p)
-    for offset in range(1, plane_count):
-        value_total = value_total + vgrad_plane[plane_peer(offset)[0]].astype(f32)
-    value_grad_ref[...] = value_total
+    for chunk, span in enumerate(spans):
+        arrive(column, chunk, vgrad_line, vgrad_send_l, vgrad_recv_l)
+        value_acc[span, :] += combine(
+            plane, chunk, line_info, vgrad_line, line_count, line * plane_count, 1,
+            vgrad_plane_out, vgrad_plane, vgrad_send_p, vgrad_recv_p)
+        arrive(plane, chunk, kgrad_plane, kgrad_send_p, kgrad_recv_p)
+        key_acc[span, :] += combine(
+            column, chunk, plane_info, kgrad_plane, plane_count, place, plane_count,
+            kgrad_line_out, kgrad_line, kgrad_send_l, kgrad_recv_l)
+
+    def finish(group, chunk, span, total, target, send_sem, recv_sem, result_ref):
+        arrive(group, chunk, target, send_sem, recv_sem)
+        sums = total[span, :]
+        for offset in range(1, group[1]):
+            sums = sums + target[group[0](offset)[0], chunk].astype(f32)
+        result_ref[span, :] = sums
+
+    for chunk, span in enumerate(spans):
+        finish(plane, chunk, span, value_acc, vgrad_plane, vgrad_send_p, vgrad_recv_p, value_grad_ref)
+        finish(column, chunk, span, key_acc, kgrad_line, kgrad_send_l, kgrad_recv_l, key_grad_ref)
     for copy in sent:
         copy.wait_send()
 
@@ -370,7 +391,8 @@
     extra = selected.shape[1] - 1
     block_rows, head_width = key_rows.shape
     heads = log_totals.shape[0]
-    tile = key_rows.shape
+    chunks = 2
+    tile = (block_rows // chunks, head_width)
     dma = pltpu.SemaphoreType.DMA
     vmem = pl.BlockSpec(memory_space=pltpu.VMEM)
     smem = pl.BlockSpec(memory_space=pltpu.SMEM)
@@ -378,7 +400,7 @@
     bf, f32 = jnp.bfloat16, jnp.float32
     shapes = (query_rows.shape, key_rows.shape, value_rows.shape)
     held = pl.pallas_call(
-        functools.partial(whole_kernel, ka_count, inner, line_count, extra),
+        functools.partial(whole_kernel, ka_count, inner, line_count, extra, chunks),
         out_shape=tuple(pltpu.VMEM(shape, f32) for shape in shapes),
         in_specs=[hbm] * 6 + [smem] * 2,
         out_specs=(vmem, vmem, vmem),
@@ -387,27 +409,27 @@
             pltpu.VMEM(query_rows.shape, bf),
             pltpu.VMEM(query_rows.shape, bf),
             pltpu.VMEM(log_totals.shape, f32),
-            pltpu.VMEM((plane_count, *tile), bf),
-            pltpu.VMEM((line_count, extra, *tile), bf),
-            pltpu.VMEM((line_count, extra, *tile), bf),
-            pltpu.VMEM((line_count, *tile), bf),
-            pltpu.VMEM((plane_count, extra, *tile), bf),
-            pltpu.VMEM((plane_count, extra, *tile), bf),
-            pltpu.VMEM((plane_count, extra, *tile), bf),
-            pltpu.VMEM((line_count, *tile), bf),
-            pltpu.VMEM((line_count, *tile), bf),
-            pltpu.VMEM((line_count, extra, *tile), bf),
-            pltpu.VMEM((plane_count, *tile), bf),
-            pltpu.VMEM((plane_count, *tile), bf),
-            pltpu.VMEM((plane_count, extra, 8, 128), jnp.int32),
-            pltpu.VMEM((line_count, extra, 8, 128), jnp.int32),
+            pltpu.VMEM((plane_count, chunks, *tile), bf),
+            pltpu.VMEM((line_count, chunks, extra, *tile), bf),
+            pltpu.VMEM((line_count, chunks, extra, *tile), bf),
+            pltpu.VMEM((line_count, chunks, *tile), bf),
+            pltpu.VMEM((plane_count, chunks, extra, *tile), bf),
+            pltpu.VMEM((plane_count, chunks, extra, *tile), bf),
+            pltpu.VMEM((plane_count, chunks, extra, *tile), bf),
+            pltpu.VMEM((line_count, chunks, *tile), bf),
+            pltpu.VMEM((line_count, chunks, *tile), bf),
+            pltpu.VMEM((line_count, chunks, extra, *tile), bf),
+            pltpu.VMEM((plane_count, chunks, *tile), bf),
+            pltpu.VMEM((plane_count, chunks, *tile), bf),
+            pltpu.VMEM((plane_count, 1, extra, 8, 128), jnp.int32),
+            pltpu.VMEM((line_count, 1, extra, 8, 128), jnp.int32),
             pltpu.VMEM((heads * block_rows, head_width), bf),
             pltpu.VMEM((heads * block_rows, head_width), bf),
             pltpu.VMEM((heads * block_rows, head_width), f32),
-            pltpu.VMEM(tile, f32),
-            pltpu.VMEM(tile, f32),
-            *[dma((count,)) for count in (plane_count, plane_count, line_count, line_count) * 5],
-            dma((6,)),
+            pltpu.VMEM(key_rows.shape, f32),
+            pltpu.VMEM(key_rows.shape, f32),
+            *[dma((count, chunks)) for count in (plane_count, plane_count, line_count, line_count) * 5],
+            dma((2 * chunks + 4,)),
         ],
         compiler_params=pltpu.CompilerParams(collective_id=0, has_side_effects=True),
     )(query_rows, key_rows, value_rows, outputs, out_grads, log_totals, selected, counts)

time: 28.8 us -> 29.5 us (1.024)
  Pallas kernels: 27.3 us -> 27.9 us
    pallas_call x1, Pallas kernels: 26.5 us -> 27.2 us  [kernel_shards(): pl.pallas_call(functools.partial(whole_kernel, ka_count, inner, line_coun...]
where the time goes in v4:
time: 29.5 us; the launch traced here: 29.2 us
  Pallas kernels  27.9 us (95%)
  between operations  1.29 us (4%)
    pallas_call x1, Pallas kernels, kernel_shards(): pl.pallas_call(functools.partial(whole_kernel, ka_count, inner, line_coun...  27.2 us
    pallas_call x1, Pallas kernels, kernel_shards(): pl.pallas_call(write_kernel, out_shape=tuple((jax.ShapeDtypeStruct(shape,...  0.77 us

profile of v4, /device:TPU:0, one launch (start us, length us, event | category | flops | bytes accessed | tf_op | source)
XLA Modules:
  0.0 29.2 jit_solution(17902624843557357096)
XLA Ops:
  1.3 27.2 %shard_map.103 = (f32[128,512]{1,0:T(8,128)S(1)}, f32[128,128]{1,0:T(8,128)S(1)}, f32[128,128]{1,0:T(8,128)S(1)}) custom-call(bf16[128,512]{1,0:T(8,128)(2,1)} %query_hbm.1, bf16[128,128]{1,0:T(8,128)(2,1)} %key_hbm.1, bf16[128,128]{1,0:T(8,128)(2,1)} %value_hbm.1, bf16[128,512]{1,0:T(8,128)(2,1)} %out_hbm.1, bf16[128,512]{1,0:T(8,128)(2,1)} %grad_hbm.1, ...), custom_call_target="tpu_custom_call" | custom-call | tf_op jit(solution)/shard_map/pallas_call | solution.py:402
  28.5 0.8 %shard_map.104 = (f32[128,512]{1,0:T(8,128)}, f32[128,128]{1,0:T(8,128)}, f32[128,128]{1,0:T(8,128)}) custom-call(f32[128,512]{1,0:T(8,128)S(1)} %get-tuple-element.6.refs_0_, f32[128,128]{1,0:T(8,128)S(1)} %get-tuple-element.7.refs_1_, f32[128,128]{1,0:T(8,128)S(1)} %get-tuple-element.8.refs_2_), custom_call_target="tpu_custom_call" | custom-call | tf_op jit(solution)/shard_map/pallas_call | solution.py:436

commit v5 on v3

--- a/solution.py
+++ b/solution.py
@@ -162,9 +162,9 @@
 
 def whole_kernel(
     ka_count, inner, line_count, extra,
-    query_hbm, key_hbm, value_hbm, out_hbm, grad_hbm, total_hbm, selected_ref, counts_ref,
+    query_hbm, key_hbm, value_hbm, out_hbm, grad_hbm, total_hbm, selected_hbm, counts_hbm,
     query_grad_ref, key_grad_ref, value_grad_ref,
-    query_ref, out_ref, grad_ref, total_ref,
+    query_ref, out_ref, grad_ref, total_ref, selected_ref, counts_ref,
     key_plane, key_line, key_line_out, value_line, value_plane, value_plane_out,
     kgrad_plane, kgrad_line, kgrad_line_out, vgrad_line, vgrad_plane, vgrad_plane_out,
     plane_info, line_info, query_stack, grad_stack, query_acc, key_acc, value_acc,
@@ -186,12 +186,22 @@
     scale = head_width ** (-0.5)
     block = line * plane_count + place
 
+    def partner(me, offset, count):
+        if count & (count - 1):
+            return lax.rem(me + offset, count)
+        peer, bit = me, 1
+        while bit < count:
+            if offset & bit:
+                peer = peer + bit - 2 * bit * lax.rem(lax.div(me, bit), 2)
+            bit *= 2
+        return peer
+
     def plane_peer(offset):
-        peer = lax.rem(place + offset, plane_count)
+        peer = partner(place, offset, plane_count)
         return peer, (line * inner + lax.div(peer, ka_count), lax.rem(peer, ka_count))
 
     def line_peer(offset):
-        peer = lax.rem(line + offset, line_count)
+        peer = partner(line, offset, line_count)
         return peer, (peer * inner + row, ka_index)
 
     plane = (plane_peer, plane_count, place)
@@ -204,6 +214,7 @@
     loads = [
         pltpu.make_async_copy(source, target, load_sem.at[index])
         for index, (source, target) in enumerate((
+            (selected_hbm, selected_ref), (counts_hbm, counts_ref),
             (key_hbm, key_plane.at[place]), (value_hbm, value_line.at[line]),
             (query_hbm, query_ref), (grad_hbm, grad_ref), (out_hbm, out_ref), (total_hbm, total_ref),
         ))
@@ -211,6 +222,8 @@
     for load in loads:
         load.start()
 
+    loads[0].wait()
+    loads[1].wait()
     targets = [
         jnp.where(slot + 1 < counts_ref[0], selected_ref[0, slot + 1], -1) for slot in range(extra)
     ]
@@ -231,7 +244,7 @@
         sent.append(copy)
 
     def spread(group, target, send_sem, recv_sem):
-        for offset in range(1, group[1]):
+        for offset in range(group[1] - 1, 0, -1):
             send(group, offset, target.at[group[2]], target, send_sem, recv_sem)
 
     def arrive(group, target, send_sem, recv_sem):
@@ -243,15 +256,15 @@
                 recv_sem=recv_sem.at[peer], device_id=device, device_id_type=MESH,
             ).wait_recv()
 
-    loads[0].wait()
-    loads[1].wait()
+    loads[2].wait()
+    loads[3].wait()
     pl.semaphore_wait(barrier, plane_count + line_count - 2)
     spread(column, line_info, info_send_l, info_recv_l)
     spread(plane, plane_info, info_send_p, info_recv_p)
     spread(column, value_line, value_send_l, value_recv_l)
     spread(plane, key_plane, key_send_p, key_recv_p)
 
-    for load in loads[2:]:
+    for load in loads[4:]:
         load.wait()
     deltas = []
     for head in range(heads):
@@ -272,7 +285,7 @@
 
     def pick(group, info, held, held_count, first, step, out, target, send_sem, recv_sem):
         peer_of, count, me = group
-        for offset in list(range(1, count)) + [0]:
+        for offset in range(count - 1, -1, -1):
             peer, _ = peer_of(offset)
             for slot in range(extra):
                 wanted = info[peer, slot][0:1, :]
@@ -331,7 +344,7 @@
 
     def combine(group, info, held, held_count, first, step, out, target, send_sem, recv_sem):
         peer_of, count, _ = group
-        for offset in list(range(1, count)) + [0]:
+        for offset in range(count - 1, -1, -1):
             peer, _ = peer_of(offset)
             sums = jnp.zeros(held.shape[2:], f32)
             for other in range(held_count):
@@ -373,20 +386,21 @@
     tile = key_rows.shape
     dma = pltpu.SemaphoreType.DMA
     vmem = pl.BlockSpec(memory_space=pltpu.VMEM)
-    smem = pl.BlockSpec(memory_space=pltpu.SMEM)
     hbm = pl.BlockSpec(memory_space=pl.ANY)
     bf, f32 = jnp.bfloat16, jnp.float32
     shapes = (query_rows.shape, key_rows.shape, value_rows.shape)
     held = pl.pallas_call(
         functools.partial(whole_kernel, ka_count, inner, line_count, extra),
         out_shape=tuple(pltpu.VMEM(shape, f32) for shape in shapes),
-        in_specs=[hbm] * 6 + [smem] * 2,
+        in_specs=[hbm] * 8,
         out_specs=(vmem, vmem, vmem),
         scratch_shapes=[
             pltpu.VMEM(query_rows.shape, bf),
             pltpu.VMEM(query_rows.shape, bf),
             pltpu.VMEM(query_rows.shape, bf),
             pltpu.VMEM(log_totals.shape, f32),
+            pltpu.SMEM(selected.shape, jnp.int32),
+            pltpu.SMEM(counts.shape, jnp.int32),
             pltpu.VMEM((plane_count, *tile), bf),
             pltpu.VMEM((line_count, extra, *tile), bf),
             pltpu.VMEM((line_count, extra, *tile), bf),
@@ -407,7 +421,7 @@
             pltpu.VMEM(tile, f32),
             pltpu.VMEM(tile, f32),
             *[dma((count,)) for count in (plane_count, plane_count, line_count, line_count) * 5],
-            dma((6,)),
+            dma((8,)),
         ],
         compiler_params=pltpu.CompilerParams(collective_id=0, has_side_effects=True),
     )(query_rows, key_rows, value_rows, outputs, out_grads, log_totals, selected, counts)

time: 28.8 us -> 27.9 us (0.969)
  Pallas kernels: 27.3 us -> 26.4 us
    pallas_call x1, Pallas kernels: 26.5 us -> 25.7 us  [kernel_shards(): pl.pallas_call(functools.partial(whole_kernel, ka_count, inner, line_coun...]
where the time goes in v5:
time: 27.9 us; the launch traced here: 27.7 us
  Pallas kernels  26.4 us (95%)
  between operations  1.29 us (5%)
    pallas_call x1, Pallas kernels, kernel_shards(): pl.pallas_call(functools.partial(whole_kernel, ka_count, inner, line_coun...  25.7 us
    pallas_call x1, Pallas kernels, kernel_shards(): pl.pallas_call(write_kernel, out_shape=tuple((jax.ShapeDtypeStruct(shape,...  0.77 us

profile of v5, /device:TPU:0, one launch (start us, length us, event | category | flops | bytes accessed | tf_op | source)
XLA Modules:
  0.0 27.7 jit_solution(10860571892356165893)
XLA Ops:
  1.3 25.7 %shard_map.103 = (f32[128,512]{1,0:T(8,128)S(1)}, f32[128,128]{1,0:T(8,128)S(1)}, f32[128,128]{1,0:T(8,128)S(1)}) custom-call(bf16[128,512]{1,0:T(8,128)(2,1)} %query_hbm.1, bf16[128,128]{1,0:T(8,128)(2,1)} %key_hbm.1, bf16[128,128]{1,0:T(8,128)(2,1)} %value_hbm.1, bf16[128,512]{1,0:T(8,128)(2,1)} %out_hbm.1, bf16[128,512]{1,0:T(8,128)(2,1)} %grad_hbm.1, ...), custom_call_target="tpu_custom_call" | custom-call | tf_op jit(solution)/shard_map/pallas_call | solution.py:392
  27.0 0.8 %shard_map.104 = (f32[128,512]{1,0:T(8,128)}, f32[128,128]{1,0:T(8,128)}, f32[128,128]{1,0:T(8,128)}) custom-call(f32[128,512]{1,0:T(8,128)S(1)} %get-tuple-element.6.refs_0_, f32[128,128]{1,0:T(8,128)S(1)} %get-tuple-element.7.refs_1_, f32[128,128]{1,0:T(8,128)S(1)} %get-tuple-element.8.refs_2_), custom_call_target="tpu_custom_call" | custom-call | tf_op jit(solution)/shard_map/pallas_call | solution.py:428
